TPU v7x, 128 devices: a whole 4x4x4 slice. The times are simulated.
128 devices in a mesh: row: 8 (over y, core), col: 16 (over z, x).
Axes of the slice: x: 4, y: 4, z: 4, core: 2. Of those that a mesh axis runs over, the one named last changes fastest.
Arguments:
- amplitudes: float32 [96, 256, 1024], P('col', None, 'row'), may hold values from -6 to 6
- interaction: float32 [16384, 16384], P('row', 'col'), may hold values from -0.5 to 0.5, as said below
- tile_counts: int32 [16], replicated, may hold values from 2 to 6, as said below
- tile_block: int32 [96], replicated, may hold values from -1 to 63, as said below
- recouple_sign: int32 [96], replicated, may hold values from 0 to 1
- orbit_perm: int32 [96, 256], replicated, may hold values from 0 to 255, each once within a row
- particle_energy: float32 [96, 256], P('col'), may hold values from -2 to 2
Outputs:
- sigma: float32 [96, 256, 1024], P('col', None, 'row')
Inputs may be any that keep to these rules, and one draw needn't show every extreme that they name: Owner c holds its live tiles in its first tile_counts[c] slots; the counts sum to 64, and some owner holds 6. `tile_block`: live slots map one to one onto the 64 cross-channel tiles, and slots that are not live hold -1; two live tiles of one owner never lie in the same aligned group of 4 cross-channel tiles. interaction equals its transpose.
All inputs are finite; a program needn't handle non-finite values.
Results may differ from a plain program's by a relative error of at most 0.000061.
Values sent between devices are 32-bit elements; how exact they have to be, the bound alone decides.
A program may use at most 128 MiB of HBM per device.

v0:
```python
import jax
import jax.numpy as jnp
from jax import lax
from jax.sharding import PartitionSpec as P


def split_up(value, dim, length):
    before, after = (value.shape[:dim], value.shape[dim + 1 :])
    return jnp.moveaxis(value.reshape(*before, length, -1, *after), dim, 0)


def sum_at_owner(value, axis, dim):
    length = lax.axis_size(axis)
    tiles = lax.all_to_all(split_up(value, dim, length), axis, 0, 0, tiled=True)
    return jnp.sum(tiles, axis=0)


def tile_recouple(tiles, phases, orders):
    moved = jax.vmap(lambda single, ordering: jnp.take(single, ordering, axis=0))(tiles, orders)
    return moved * phases[:, None, None]


def local(
    amplitudes, interaction, tile_counts, tile_block, recouple_sign, orbit_perm, particle_energy
):
    column_index = lax.axis_index("col")
    row_index = lax.axis_index("row")
    column_count = lax.axis_size("col")
    slots, tile_rows, narrow_cols = amplitudes.shape
    row_blocks = interaction.shape[0] // tile_rows
    col_blocks = interaction.shape[1] // tile_rows
    tile_total = tile_block.shape[0]
    slot_ids = jnp.arange(slots, dtype=jnp.int32)
    is_live = slot_ids < jnp.take(tile_counts, column_index)
    live_mask = is_live.astype(jnp.float32)[:, None, None]
    own_block = jnp.where(
        is_live, lax.dynamic_slice_in_dim(tile_block, column_index * slots, slots), -1
    )
    all_phases = (1 - 2 * recouple_sign).astype(jnp.float32)
    own_phases = lax.dynamic_slice_in_dim(all_phases, column_index * slots, slots)
    own_orders = lax.dynamic_slice_in_dim(orbit_perm, column_index * slots, slots, 0)
    diagonal = particle_energy[:, :, None] * amplitudes
    tile_ids = jnp.arange(tile_total, dtype=jnp.int32)
    peer_ids = jnp.arange(column_count, dtype=jnp.int32)

    def tiles_of(blocks):
        matches = tile_block[None, :] == blocks[:, None]
        return jnp.sum(jnp.where(matches, tile_ids[None, :], 0), axis=1)

    target_col = own_block // col_blocks
    my_blocks = column_index * col_blocks + jnp.arange(col_blocks, dtype=jnp.int32)
    block_tiles = tiles_of(my_blocks)
    widened = lax.all_gather(amplitudes, "row", axis=2, tiled=True)
    widened = tile_recouple(widened, own_phases, own_orders)
    group_blocks = row_index * row_blocks + jnp.arange(row_blocks, dtype=jnp.int32)
    group_tiles = tiles_of(group_blocks)
    is_owned = group_tiles // slots == column_index
    placed = (
        jnp.take(widened, group_tiles % slots, axis=0) * is_owned.astype(jnp.float32)[:, None, None]
    )
    crossed = lax.psum(placed.reshape(row_blocks * tile_rows, widened.shape[2]), "col")
    partial_cols = lax.dot_general(
        interaction,
        crossed,
        (((0,), (0,)), ((), ())),
        precision=lax.Precision.HIGHEST,
        preferred_element_type=jnp.float32,
    )
    own_part = sum_at_owner(partial_cols, "row", 1)
    blocks_here = own_part.reshape(col_blocks, tile_rows, narrow_cols)
    block_inverse = jnp.argsort(jnp.take(orbit_perm, block_tiles, axis=0), axis=1)
    blocks_here = tile_recouple(blocks_here, jnp.take(all_phases, block_tiles), block_inverse)
    block_owner = block_tiles // slots
    choose_mask = block_owner[None, :] == peer_ids[:, None]
    choose_block = jnp.sum(
        jnp.where(choose_mask, jnp.arange(col_blocks, dtype=jnp.int32)[None, :], 0), axis=1
    )
    choose_weight = jnp.max(choose_mask.astype(jnp.float32), axis=1)
    outgoing = jnp.take(blocks_here, choose_block, axis=0) * choose_weight[:, None, None]
    arrived = lax.all_to_all(outgoing, "col", split_axis=0, concat_axis=0, tiled=True)
    returned = jnp.take(arrived, jnp.clip(target_col, 0, column_count - 1), axis=0)
    return (returned + diagonal) * live_mask


def solution(mesh):
    placed = (P("col", None, "row"), P("row", "col"), P(), P(), P(), P(), P("col", None))
    return jax.shard_map(
        local, mesh=mesh, in_specs=placed, out_specs=P("col", None, "row"), check_vma=False
    )
```

profile of v0, /device:TPU:0, one launch (start us, length us, event | category | flops | bytes accessed | tf_op | source)
XLA Modules:
  0.0 393.0 jit_solution(7255663869322990882)
XLA Ops:
  7.4 0.7 all-gather.2.cloned.1.call-update
  8.9 0.7 bitcast_or_fusion
  9.6 0.8 select_reduce_fusion
  10.7 0.7 compare_and_fusion
  11.4 45.4 %all-gather.2.cloned.1.call-done = f32[6,256,1024]{2,1,0:T(8,128)} async-done(((f32[6,256,128]{2,1,0:T(8,128)}), f32[6,256,1024]{2,1,0:T(8,128)}) %all-gather.2.cloned.1.call-update) | async-done | bytes 6291472 | tf_op jit(solution)/shard_map/all_gather | solution.py:53
  56.8 30.5 %gather_fusion.5 = f32[1536,1024]{1,0:T(8,128)} fusion(f32[6,256,1024]{2,1,0:T(8,128)} %all-gather.2.cloned.1.call-done, s32[1536]{0:T(1024)S(1)} %reshape.221), kind=kCustom, calls=%fused_computation.5 | custom fusion | bytes 12595200 | tf_op jit(solution)/shard_map/vmap(jit(_take))/gather | solution.py:19
  87.3 4.9 %select_multiply_fusion = f32[6,256,1024]{2,1,0:T(8,128)} fusion(f32[6,256,1024]{2,1,0:T(8,128)} %bitcast.45, f32[6]{0:T(128)S(1)} %dynamic_slice.11, pred[6,256]{1,0:T(8,128)(4,1)S(1)} %compare_and_fusion), kind=kLoop, calls=%fused_computation.9 | loop fusion | flops 3145728 | bytes 12584472 | tf_op jit(solution)/shard_map/mul | solution.py:20
  92.2 7.1 %gather_fusion.1 = f32[8,256,1024]{2,1,0:T(8,128)} fusion(f32[6,256,1024]{2,1,0:T(8,128)} %select_multiply_fusion, s32[1024]{0:T(1024)S(1)} %pad_clamp_fusion.2), kind=kCustom, calls=%fused_computation.1 | custom fusion | bytes 16777248 | tf_op jit(solution)/shard_map/jit(_take)/gather | solution.py:59
  99.3 5.8 %fusion = f32[2048,1024]{1,0:T(8,128)} fusion(f32[8,256,1024]{2,1,0:T(8,128)} %gather_fusion.1, f32[2048]{0:T(1024)S(1)} %bitcast.48, pred[2048]{0:T(1024)(128)(4,1)S(1)} %broadcast_in_dim.145), kind=kLoop, calls=%fused_computation.8 | loop fusion | flops 4194304 | bytes 16787456 | tf_op jit(solution)/shard_map/mul | solution.py:59
  105.1 142.9 %all-reduce.2.cloned.1.call-done = f32[2048,1024]{1,0:T(8,128)} async-done(((f32[2048,1024]{1,0:T(8,128)}), f32[2048,1024]{1,0:T(8,128)}) %all-reduce.2.cloned.1.call-update) | async-done | bytes 8388624 | tf_op jit(solution)/shard_map/psum | solution.py:61
  248.1 31.6 %fusion.5 = f32[1024,1024]{1,0:T(8,128)} fusion(f32[2048,1024]{1,0:T(8,128)} %all-reduce.2.cloned.1.call-done, f32[2048,1024]{1,0:T(8,128)} %param.8), kind=kOutput, calls=%fused_computation.61 | convolution fusion | flops 25769803776 | bytes 20971520 | tf_op jit(solution)/shard_map/dot_general | solution.py:62
  279.7 4.7 %all-to-all-start = ((f32[8,1024,128]{1,2,0:T(8,128)}), f32[8,1024,128]{1,2,0:T(8,128)}, u32[]{:S(2)}, u32[]{:S(2)}) async-start(f32[8,1024,128]{1,2,0:T(8,128)} %bitcast.46), calls=%async_computation | async-start | bytes 8388608 | tf_op jit(solution)/shard_map/all_to_all | solution.py:14
  285.5 1.5 gather_fusion
  288.4 2.7 sort.19.cloned.1.call-done
  291.1 0.7 fusion.1
  292.5 41.5 %all-to-all-done = f32[8,1024,128]{1,2,0:T(8,128)} async-done(((f32[8,1024,128]{1,2,0:T(8,128)}), f32[8,1024,128]{1,2,0:T(8,128)}, u32[]{:S(2)}, u32[]{:S(2)}) %all-to-all-start) | async-done | bytes 4194336 | tf_op jit(solution)/shard_map/all_to_all | solution.py:14
  334.0 2.6 reduce_sum.44
  336.8 6.8 %gather_fusion.6 = f32[1024,128]{1,0:T(8,128)S(1)} fusion(f32[4,256,128]{2,1,0:T(8,128)S(1)} %bitcast.44, s32[1024]{0:T(1024)S(1)} %bitcast.43), kind=kCustom, calls=%fused_computation.6 | custom fusion | bytes 1056768 | tf_op jit(solution)/shard_map/vmap(jit(_take))/gather | solution.py:19
  343.9 0.7 gather_fusion.3
  344.6 1.6 select_multiply_fusion.1
  346.2 4.5 %all-to-all-start.1 = ((f32[16,256,128]{2,1,0:T(8,128)}), f32[16,256,128]{2,1,0:T(8,128)S(1)}, u32[]{:S(2)}, u32[]{:S(2)}) async-start(f32[16,256,128]{2,1,0:T(8,128)} %select_multiply_fusion.1), calls=%async_computation.1 | async-start | bytes 4194304 | tf_op jit(solution)/shard_map/all_to_all | solution.py:80
  352.1 29.7 %all-to-all-done.1 = f32[16,256,128]{2,1,0:T(8,128)S(1)} async-done(((f32[16,256,128]{2,1,0:T(8,128)}), f32[16,256,128]{2,1,0:T(8,128)S(1)}, u32[]{:S(2)}, u32[]{:S(2)}) %all-to-all-start.1) | async-done | bytes 2097184 | tf_op jit(solution)/shard_map/all_to_all | solution.py:80
  381.8 1.5 gather_fusion.4
  383.2 2.3 add_multiply_fusion
  (45 shorter events, 5.4 us)
Async XLA Ops:
  7.4 49.4 %all-gather.2.cloned.1.call-start = ((), (), s32[]{:S(2)}) async-start(), calls=%async_computation.2 | async-start | bytes 7077888 | tf_op jit(solution)/shard_map/all_gather | solution.py:53
  8.1 240.0 %all-reduce.2.cloned.1.call-start = ((), (), s32[]{:S(2)}) async-start(), calls=%async_computation.3 | async-start | bytes 16777216 | tf_op jit(solution)/shard_map/psum | solution.py:61
  279.7 4.9 %copy-start.2 = (s32[96]{0:T(128)S(1)}, s32[96]{0:T(128)}, u32[]{:S(2)}) copy-start(s32[96]{0:T(128)} %param.10) | copy-start | bytes 1156
  279.7 54.3 %all-to-all-start = ((f32[8,1024,128]{1,2,0:T(8,128)}), f32[8,1024,128]{1,2,0:T(8,128)}, u32[]{:S(2)}, u32[]{:S(2)}) async-start(f32[8,1024,128]{1,2,0:T(8,128)} %bitcast.46), calls=%async_computation | async-start | bytes 8388608 | tf_op jit(solution)/shard_map/all_to_all | solution.py:14
  284.4 6.7 %sort.19.cloned.1.call-start = ((), (), s32[]{:S(2)}) async-start(), calls=%async_computation.4 | async-start | bytes 24608 | tf_op jit(solution)/shard_map/jit(argsort)/sort | solution.py:71
  343.8 6.9 %copy-start.3 = (s32[16]{0:T(128)S(1)}, s32[16]{0:T(128)}, u32[]{:S(2)}) copy-start(s32[16]{0:T(128)} %param.9) | copy-start | bytes 196
  343.9 39.4 %copy-start = (f32[6,256,128]{2,1,0:T(8,128)S(1)}, f32[6,256,128]{2,1,0:T(8,128)}, u32[]{:S(2)}) copy-start(f32[6,256,128]{2,1,0:T(8,128)} %param.7) | copy-start | bytes 2359300
  343.9 39.4 %copy-start.1 = (f32[6,256]{1,0:T(8,128)S(1)}, f32[6,256]{1,0:T(8,128)}, u32[]{:S(2)}) copy-start(f32[6,256]{1,0:T(8,128)} %param.13) | copy-start | bytes 18436
  346.2 35.5 %all-to-all-start.1 = ((f32[16,256,128]{2,1,0:T(8,128)}), f32[16,256,128]{2,1,0:T(8,128)S(1)}, u32[]{:S(2)}, u32[]{:S(2)}) async-start(f32[16,256,128]{2,1,0:T(8,128)} %select_multiply_fusion.1), calls=%async_computation.1 | async-start | bytes 4194304 | tf_op jit(solution)/shard_map/all_to_all | solution.py:80
Sparse Core Ops, SparseCore 0:
  9.8 46.9 all-gather.1
  105.3 142.7 all-reduce.1
Sparse Core Ops, SparseCore 1:
  288.3 2.5 sort.21.cloned.1.call-done
  (1 shorter events, 0.0 us)
where the time goes:
time: 394 us; the launch traced here: 393 us
  waiting for transfers between devices  260 us (66%)
  local copies, waits for them, and re-layouts  53.2 us (14%)
  matrix products  31.6 us (8%)
  other arithmetic  23.1 us (6%)
  between operations  15.6 us (4%)
  starting transfers between devices  9.24 us (2%)
    psum x1, waiting for transfers between devices, local(): lax.psum(placed.reshape(row_blocks * tile_rows, widened.shape[2]), 'col')  143 us
    all_gather x1, waiting for transfers between devices, local(): widened = lax.all_gather(amplitudes, 'row', axis=2, tiled=True)  45.4 us
    all_to_all x1, waiting for transfers between devices, sum_at_owner(): tiles = lax.all_to_all(split_up(value, dim, length), axis, 0, 0, tiled=True)  41.5 us
    gather x3, local copies, waits for them, and re-layouts, tile_recouple(): jnp.take(single, ordering, axis=0)  37.3 us
    dot_general x1, matrix products, local(): lax.dot_general(interaction, crossed, (((0,), (0,)), ((), ())), precision...  31.6 us
    all_to_all x1, waiting for transfers between devices, local(): lax.all_to_all(outgoing, 'col', split_axis=0, concat_axis=0, tiled=True)  29.7 us
  transfers between devices with their start and end apart: 4, of which 4 were waited for; matrix products, arithmetic and copies ran while one was open for 2% of the time, Pallas kernels for 0%

commit v1 on v0

--- a/solution.py
+++ b/solution.py
@@ -2,6 +2,28 @@
 import jax.numpy as jnp
 from jax import lax
 from jax.sharding import PartitionSpec as P
+
+
+def in_order(blocks, dim):
+    blocks = jnp.moveaxis(blocks, 0, dim)
+    shape = blocks.shape
+    return blocks.reshape(*shape[:dim], shape[dim] * shape[dim + 1], *shape[dim + 2 :])
+
+
+def gather_around(shard, axis, dim):
+    count = lax.axis_size(axis)
+    pairs = [(i, (i + 1) % count) for i in range(count)]
+    back = [(b, a) for a, b in pairs]
+    lower, upper = ([], [])
+    for step in range(count - 1):
+        if step % 2 == 0:
+            lower.append(lax.ppermute(lower[-1] if lower else shard, axis, pairs))
+        else:
+            upper.append(lax.ppermute(upper[-1] if upper else shard, axis, back))
+    parts = jnp.stack([*lower[::-1], shard, *upper])
+    shift = lax.axis_index(axis) - len(lower)
+    parts = parts[(jnp.arange(count) - shift) % count]
+    return in_order(parts, dim)
 
 
 def split_up(value, dim, length):
@@ -50,7 +72,7 @@
     target_col = own_block // col_blocks
     my_blocks = column_index * col_blocks + jnp.arange(col_blocks, dtype=jnp.int32)
     block_tiles = tiles_of(my_blocks)
-    widened = lax.all_gather(amplitudes, "row", axis=2, tiled=True)
+    widened = gather_around(amplitudes, "row", 2)
     widened = tile_recouple(widened, own_phases, own_orders)
     group_blocks = row_index * row_blocks + jnp.arange(row_blocks, dtype=jnp.int32)
     group_tiles = tiles_of(group_blocks)

time: 394 us -> 418 us (1.061)
  local copies, waits for them, and re-layouts: 53.2 us -> 76.9 us
  waiting for transfers between devices: 260 us -> 251 us
  starting transfers between devices: 9.24 us -> 18.2 us
    all_gather x1 -> x0, waiting for transfers between devices: 45.4 us -> none  [local(): widened = lax.all_gather(amplitudes, 'row', axis=2, tiled=True)]
    ppermute x0 -> x7, waiting for transfers between devices: none -> 37.7 us  [the longest x4 37.2 us: gather_around(): lower.append(lax.ppermute(lower[-1] if lower else shard, axis, pairs))]
    unnamed x12 -> x19, local copies, waits for them, and re-layouts: 0.12 us -> 10.1 us
    ppermute x0 -> x7, starting transfers between devices: none -> 9.13 us  [the longest x3 9.12 us: gather_around(): upper.append(lax.ppermute(upper[-1] if upper else shard, axis, back))]
    gather x0 -> x1, local copies, waits for them, and re-layouts: none -> 6.38 us  [gather_around(): parts = parts[(jnp.arange(count) - shift) % count]]
    reshape x0 -> x1, local copies, waits for them, and re-layouts: none -> 6.33 us  [in_order(): blocks.reshape(*shape[:dim], shape[dim] * shape[dim + 1], *shape[dim + 2:])]
  transfers between devices with their start and end apart: 4 -> 10, of which waited for: 4 -> 8; matrix products, arithmetic and copies ran while one was open for 2% -> 5% of each run, Pallas kernels for 0% -> 0%
where the time goes in v1:
time: 418 us; the launch traced here: 417 us
  waiting for transfers between devices  251 us (60%)
  local copies, waits for them, and re-layouts  76.9 us (18%)
  matrix products  31.7 us (8%)
  other arithmetic  23.6 us (6%)
  starting transfers between devices  18.2 us (4%)
  between operations  15.7 us (4%)
    psum x1, waiting for transfers between devices, local(): lax.psum(placed.reshape(row_blocks * tile_rows, widened.shape[2]), 'col')  142 us
    all_to_all x1, waiting for transfers between devices, sum_at_owner(): tiles = lax.all_to_all(split_up(value, dim, length), axis, 0, 0, tiled=True)  41.7 us
    gather x3, local copies, waits for them, and re-layouts, tile_recouple(): jnp.take(single, ordering, axis=0)  37.2 us
    ppermute x4, waiting for transfers between devices, gather_around(): lower.append(lax.ppermute(lower[-1] if lower else shard, axis, pairs))  37.2 us
    dot_general x1, matrix products, local(): lax.dot_general(interaction, crossed, (((0,), (0,)), ((), ())), precision...  31.7 us
    all_to_all x1, waiting for transfers between devices, local(): lax.all_to_all(outgoing, 'col', split_axis=0, concat_axis=0, tiled=True)  29.7 us
    unnamed x19, local copies, waits for them, and re-layouts  10.1 us
    ppermute x3, starting transfers between devices, gather_around(): upper.append(lax.ppermute(upper[-1] if upper else shard, axis, back))  9.12 us
  transfers between devices with their start and end apart: 10, of which 8 were waited for; matrix products, arithmetic and copies ran while one was open for 5% of the time, Pallas kernels for 0%

profile of v1, /device:TPU:0, one launch (start us, length us, event | category | flops | bytes accessed | tf_op | source)
XLA Modules:
  0.0 417.1 jit_solution(15846877001138141068)
XLA Ops:
  7.4 3.0 collective-permute-start.4
  10.3 9.9 %collective-permute-done = f32[6,256,128]{2,1,0:T(8,128)S(1)} collective-permute-done((f32[6,256,128]{2,1,0:T(8,128)}, f32[6,256,128]{2,1,0:T(8,128)S(1)}, u32[]{:S(2)}, u32[]{:S(2)}) %collective-permute-start) | collective-permute-done | bytes 786464 | tf_op jit(solution)/shard_map/ppermute | solution.py:20
  23.2 9.6 %collective-permute-done.1 = f32[6,256,128]{2,1,0:T(8,128)S(1)} collective-permute-done((f32[6,256,128]{2,1,0:T(8,128)S(1)}, f32[6,256,128]{2,1,0:T(8,128)S(1)}, u32[]{:S(2)}, u32[]{:S(2)}) %collective-permute-start.1) | collective-permute-done | bytes 786464 | tf_op jit(solution)/shard_map/ppermute | solution.py:20
  33.9 2.9 collective-permute-start.5
  36.8 8.7 %collective-permute-done.2 = f32[6,256,128]{2,1,0:T(8,128)} collective-permute-done((f32[6,256,128]{2,1,0:T(8,128)S(1)}, f32[6,256,128]{2,1,0:T(8,128)}, u32[]{:S(2)}, u32[]{:S(2)}) %collective-permute-start.2) | collective-permute-done | bytes 786464 | tf_op jit(solution)/shard_map/ppermute | solution.py:20
  46.3 3.2 collective-permute-start.6
  49.6 9.0 %collective-permute-done.3 = f32[6,256,128]{2,1,0:T(8,128)} collective-permute-done((f32[6,256,128]{2,1,0:T(8,128)}, f32[6,256,128]{2,1,0:T(8,128)}, u32[]{:S(2)}, u32[]{:S(2)}) %collective-permute-start.3) | collective-permute-done | bytes 786464 | tf_op jit(solution)/shard_map/ppermute | solution.py:20
  66.4 2.1 bitcast_dynamic-update-slice_fusion.1
  69.5 6.4 %gather_fusion.1 = f32[8,6,256,128]{3,2,1,0:T(8,128)} fusion(f32[8,6,256,128]{3,2,1,0:T(8,128)} %bitcast_dynamic-update-slice_fusion, s32[1024]{0:T(1024)S(1)} %pad_clamp_fusion.3), kind=kCustom, calls=%fused_computation.1 | custom fusion | bytes 12582944 | tf_op jit(solution)/shard_map/gather | solution.py:25
  75.9 6.3 %copy_bitcast_fusion = f32[6,256,1024]{2,1,0:T(8,128)} fusion(f32[8,6,256,128]{3,2,1,0:T(8,128)} %gather_fusion.1), kind=kLoop, calls=%fused_computation.10 | loop fusion | bytes 12582912 | tf_op jit(solution)/shard_map/reshape | solution.py:10
  82.2 30.4 %gather_fusion.6 = f32[1536,1024]{1,0:T(8,128)} fusion(f32[6,256,1024]{2,1,0:T(8,128)} %copy_bitcast_fusion, s32[1536]{0:T(1024)S(1)} %reshape.282), kind=kCustom, calls=%fused_computation.6 | custom fusion | bytes 12595200 | tf_op jit(solution)/shard_map/vmap(jit(_take))/gather | solution.py:41
  112.6 4.8 %select_multiply_fusion = f32[6,256,1024]{2,1,0:T(8,128)} fusion(f32[6,256,1024]{2,1,0:T(8,128)} %bitcast.69, f32[6]{0:T(128)S(1)} %dynamic_slice.11, pred[6,256]{1,0:T(8,128)(4,1)S(1)} %compare_and_fusion), kind=kLoop, calls=%fused_computation.11 | loop fusion | flops 3145728 | bytes 12584472 | tf_op jit(solution)/shard_map/mul | solution.py:42
  117.4 7.1 %gather_fusion.2 = f32[8,256,1024]{2,1,0:T(8,128)} fusion(f32[6,256,1024]{2,1,0:T(8,128)} %select_multiply_fusion, s32[1024]{0:T(1024)S(1)} %get-tuple-element.25), kind=kCustom, calls=%fused_computation.2 | custom fusion | bytes 16777248 | tf_op jit(solution)/shard_map/jit(_take)/gather | solution.py:81
  124.5 5.8 %fusion = f32[2048,1024]{1,0:T(8,128)} fusion(f32[8,256,1024]{2,1,0:T(8,128)} %gather_fusion.2, f32[2048]{0:T(1024)S(1)} %bitcast.72, pred[2048]{0:T(1024)(128)(4,1)S(1)} %broadcast_in_dim.146), kind=kLoop, calls=%fused_computation.9 | loop fusion | flops 4194304 | bytes 16787456 | tf_op jit(solution)/shard_map/mul | solution.py:81
  130.3 142.0 %all-reduce.2.cloned.1.call-done = f32[2048,1024]{1,0:T(8,128)} async-done(((f32[2048,1024]{1,0:T(8,128)}), f32[2048,1024]{1,0:T(8,128)}) %all-reduce.2.cloned.1.call-update) | async-done | bytes 8388624 | tf_op jit(solution)/shard_map/psum | solution.py:83
  272.3 31.7 %fusion.7 = f32[1024,1024]{1,0:T(8,128)} fusion(f32[2048,1024]{1,0:T(8,128)} %all-reduce.2.cloned.1.call-done, f32[2048,1024]{1,0:T(8,128)} %param.8), kind=kOutput, calls=%fused_computation.78 | convolution fusion | flops 25769803776 | bytes 20971520 | tf_op jit(solution)/shard_map/dot_general | solution.py:84
  304.0 4.6 %all-to-all-start = ((f32[8,1024,128]{1,2,0:T(8,128)}), f32[8,1024,128]{1,2,0:T(8,128)}, u32[]{:S(2)}, u32[]{:S(2)}) async-start(f32[8,1024,128]{1,2,0:T(8,128)} %bitcast.70), calls=%async_computation | async-start | bytes 8388608 | tf_op jit(solution)/shard_map/all_to_all | solution.py:36
  312.3 2.8 sort.19.cloned.1.call-done
  316.5 41.7 %all-to-all-done = f32[8,1024,128]{1,2,0:T(8,128)} async-done(((f32[8,1024,128]{1,2,0:T(8,128)}), f32[8,1024,128]{1,2,0:T(8,128)}, u32[]{:S(2)}, u32[]{:S(2)}) %all-to-all-start) | async-done | bytes 4194336 | tf_op jit(solution)/shard_map/all_to_all | solution.py:36
  358.2 2.6 reduce_sum.44
  361.0 6.8 %gather_fusion.7 = f32[1024,128]{1,0:T(8,128)S(1)} fusion(f32[4,256,128]{2,1,0:T(8,128)S(1)} %bitcast.68, s32[1024]{0:T(1024)S(1)} %bitcast.67), kind=kCustom, calls=%fused_computation.7 | custom fusion | bytes 1056768 | tf_op jit(solution)/shard_map/vmap(jit(_take))/gather | solution.py:41
  370.4 4.5 %all-to-all-start.1 = ((f32[16,256,128]{2,1,0:T(8,128)}), f32[16,256,128]{2,1,0:T(8,128)S(1)}, u32[]{:S(2)}, u32[]{:S(2)}) async-start(f32[16,256,128]{2,1,0:T(8,128)} %select_multiply_fusion.1), calls=%async_computation.1 | async-start | bytes 4194304 | tf_op jit(solution)/shard_map/all_to_all | solution.py:102
  376.3 29.7 %all-to-all-done.1 = f32[16,256,128]{2,1,0:T(8,128)S(1)} async-done(((f32[16,256,128]{2,1,0:T(8,128)}), f32[16,256,128]{2,1,0:T(8,128)S(1)}, u32[]{:S(2)}, u32[]{:S(2)}) %all-to-all-start.1) | async-done | bytes 2097184 | tf_op jit(solution)/shard_map/all_to_all | solution.py:102
  407.4 2.3 add_multiply_fusion
  (67 shorter events, 23.6 us)
Async XLA Ops:
  7.4 57.2 %copy-start = (f32[6,256,128]{2,1,0:T(8,128)S(1)}, f32[6,256,128]{2,1,0:T(8,128)}, u32[]{:S(2)}) copy-start(f32[6,256,128]{2,1,0:T(8,128)} %param.7) | copy-start | bytes 2359300
  7.4 265.0 %all-reduce.2.cloned.1.call-start = ((), (), s32[]{:S(2)}) async-start(), calls=%async_computation.2 | async-start | bytes 16777216 | tf_op jit(solution)/shard_map/psum | solution.py:83
  7.4 12.8 %collective-permute-start = (f32[6,256,128]{2,1,0:T(8,128)}, f32[6,256,128]{2,1,0:T(8,128)S(1)}, u32[]{:S(2)}, u32[]{:S(2)}) collective-permute-start(f32[6,256,128]{2,1,0:T(8,128)} %param.7), channel_id=1, source_target_pairs={{0,16},{16,32},{32,48},{48,64},{64,80},{80,96},{96,112},{112,0},{1... | collective-permute-start | bytes 2359304 | tf_op jit(solution)/shard_map/ppermute | solution.py:20
  7.4 26.5 %collective-permute-start.4 = (f32[6,256,128]{2,1,0:T(8,128)}, f32[6,256,128]{2,1,0:T(8,128)S(1)}, u32[]{:S(2)}, u32[]{:S(2)}) collective-permute-start(f32[6,256,128]{2,1,0:T(8,128)} %param.7), channel_id=1, source_target_pairs={{16,0},{32,16},{48,32},{64,48},{80,64},{96,80},{112,96},{0,112},{1... | collective-permute-start | bytes 2359304 | tf_op jit(solution)/shard_map/ppermute | solution.py:22
  20.2 12.6 %collective-permute-start.1 = (f32[6,256,128]{2,1,0:T(8,128)S(1)}, f32[6,256,128]{2,1,0:T(8,128)S(1)}, u32[]{:S(2)}, u32[]{:S(2)}) collective-permute-start(f32[6,256,128]{2,1,0:T(8,128)S(1)} %collective-permute-done), channel_id=1, source_target_pairs={{0,16},{16,32},{32,48},{48,64},{64,80},{80,96},{96,112},{112,0},{1... | collective-permute-start | bytes 2359304 | tf_op jit(solution)/shard_map/ppermute | solution.py:20
  32.8 12.7 %collective-permute-start.2 = (f32[6,256,128]{2,1,0:T(8,128)S(1)}, f32[6,256,128]{2,1,0:T(8,128)}, u32[]{:S(2)}, u32[]{:S(2)}) collective-permute-start(f32[6,256,128]{2,1,0:T(8,128)S(1)} %collective-permute-done.1), channel_id=1, source_target_pairs={{0,16},{16,32},{32,48},{48,64},{64,80},{80,96},{96,112},{112,0},{1... | collective-permute-start | bytes 2359304 | tf_op jit(solution)/shard_map/ppermute | solution.py:20
  33.9 12.5 %collective-permute-start.5 = (f32[6,256,128]{2,1,0:T(8,128)S(1)}, f32[6,256,128]{2,1,0:T(8,128)}, u32[]{:S(2)}, u32[]{:S(2)}) collective-permute-start(f32[6,256,128]{2,1,0:T(8,128)S(1)} %collective-permute-done.4), channel_id=1, source_target_pairs={{16,0},{32,16},{48,32},{64,48},{80,64},{96,80},{112,96},{0,112},{1... | collective-permute-start | bytes 2359304 | tf_op jit(solution)/shard_map/ppermute | solution.py:22
  45.6 12.9 %collective-permute-start.3 = (f32[6,256,128]{2,1,0:T(8,128)}, f32[6,256,128]{2,1,0:T(8,128)}, u32[]{:S(2)}, u32[]{:S(2)}) collective-permute-start(f32[6,256,128]{2,1,0:T(8,128)} %collective-permute-done.2), channel_id=1, source_target_pairs={{0,16},{16,32},{32,48},{48,64},{64,80},{80,96},{96,112},{112,0},{1... | collective-permute-start | bytes 2359304 | tf_op jit(solution)/shard_map/ppermute | solution.py:20
  46.3 22.2 %collective-permute-start.6 = (f32[6,256,128]{2,1,0:T(8,128)}, f32[6,256,128]{2,1,0:T(8,128)S(1)}, u32[]{:S(2)}, u32[]{:S(2)}) collective-permute-start(f32[6,256,128]{2,1,0:T(8,128)} %collective-permute-done.5), channel_id=1, source_target_pairs={{16,0},{32,16},{48,32},{64,48},{80,64},{96,80},{112,96},{0,112},{1... | collective-permute-start | bytes 2359304 | tf_op jit(solution)/shard_map/ppermute | solution.py:22
  304.0 54.2 %all-to-all-start = ((f32[8,1024,128]{1,2,0:T(8,128)}), f32[8,1024,128]{1,2,0:T(8,128)}, u32[]{:S(2)}, u32[]{:S(2)}) async-start(f32[8,1024,128]{1,2,0:T(8,128)} %bitcast.70), calls=%async_computation | async-start | bytes 8388608 | tf_op jit(solution)/shard_map/all_to_all | solution.py:36
  308.5 6.6 %sort.19.cloned.1.call-start = ((), (), s32[]{:S(2)}) async-start(), calls=%async_computation.3 | async-start | bytes 24608 | tf_op jit(solution)/shard_map/jit(argsort)/sort | solution.py:93
  368.0 6.9 %copy-start.3 = (s32[16]{0:T(128)S(1)}, s32[16]{0:T(128)}, u32[]{:S(2)}) copy-start(s32[16]{0:T(128)} %param.9) | copy-start | bytes 196
  368.0 8.1 %copy-start.2 = (s32[96]{0:T(128)S(1)}, s32[96]{0:T(128)}, u32[]{:S(2)}) copy-start(s32[96]{0:T(128)} %param.10) | copy-start | bytes 1156
  368.0 39.4 %copy-start.1 = (f32[6,256]{1,0:T(8,128)S(1)}, f32[6,256]{1,0:T(8,128)}, u32[]{:S(2)}) copy-start(f32[6,256]{1,0:T(8,128)} %param.13) | copy-start | bytes 18436
  370.4 35.5 %all-to-all-start.1 = ((f32[16,256,128]{2,1,0:T(8,128)}), f32[16,256,128]{2,1,0:T(8,128)S(1)}, u32[]{:S(2)}, u32[]{:S(2)}) async-start(f32[16,256,128]{2,1,0:T(8,128)} %select_multiply_fusion.1), calls=%async_computation.1 | async-start | bytes 4194304 | tf_op jit(solution)/shard_map/all_to_all | solution.py:102
Sparse Core Ops, SparseCore 0:
  130.5 141.8 all-reduce.1
Sparse Core Ops, SparseCore 1:
  312.3 2.5 sort.21.cloned.1.call-done
  (1 shorter events, 0.0 us)
